TPU v7x, 768 devices: a whole 4x8x12 slice. The times are simulated.
768 devices in a mesh: sec: 3 (over z_hi), tp: 64 (over z_lo, y, core), blk: 4 (over x).
Axes of the slice: x: 4, y: 8, z: 12 (z_hi: 3, z_lo: 4; z = z_hi * 4 + z_lo), core: 2. Of those that a mesh axis runs over, the one named last changes fastest.
Arguments:
- perambulator: bfloat16 [64, 2, 2048, 2048], P('tp', None, 'blk'), may hold values from -0.125 to 0.125
- backward: bfloat16 [64, 2, 2048, 2048], P('tp', None, None, 'blk'), may hold values from -0.125 to 0.125
- elementals: bfloat16 [3, 64, 2, 2048, 128], P('sec', 'tp', None, 'blk'), may hold values from -6 to 6
- diagrams: int32 [64, 16, 2], P('tp'), may hold values from 0 to 63
- owner_loads: int32 [64], P('tp'), may hold values from 1 to 16, as said below
Outputs:
- hadron: float32 [3, 64, 2, 128, 128], P('sec', 'tp', None, 'blk')
Inputs may be any that keep to these rules, and one draw needn't show every extreme that they name: `diagrams`: pair indices of each owner's slots; slots at or past the owner's load are ignored. `owner_loads`: some owner has exactly 16 live slots.
All inputs are finite; a program needn't handle non-finite values.
Results may differ from a plain program's by a relative error of at most 0.007.
Values may be sent and summed in bfloat16 or wider, within the bound.
No kernel may reach another device: no remote copies, remote signals or barrier semaphores. Data moves between devices by JAX's collectives and lax.ppermute only.
A program may use at most 64 MiB of HBM per device.

v0:
```python
import jax
import jax.numpy as jnp
from jax import lax
from jax.experimental import pallas as pl
from jax.experimental.pallas import tpu as pltpu
from jax.sharding import Mesh
from jax.sharding import PartitionSpec as P


TP = ("z", "y", "c")
BF16 = jnp.bfloat16
F32 = jnp.float32
VMEM = pl.BlockSpec(memory_space=pltpu.VMEM)
HBM = pl.BlockSpec(memory_space=pltpu.HBM)
SMEM = pl.BlockSpec(memory_space=pltpu.SMEM)


def dot(a, b, ca, cb):
    return lax.dot_general(a, b, (((ca,), (cb,)), ((), ())), preferred_element_type=F32)


def spread_kernel(
    tile_hbm, lists_hbm, load_ref, out_ref, meta_ref, tile_ref, lists_ref, sems
):
    tile_copy = pltpu.make_async_copy(tile_hbm, tile_ref, sems.at[0])
    lists_copy = pltpu.make_async_copy(lists_hbm, lists_ref, sems.at[1])
    tile_copy.start()
    lists_copy.start()
    lists_copy.wait()
    sides, slots = lists_ref.shape
    lists = lists_ref[...].astype(F32)
    lists = jnp.concatenate([lists, jnp.zeros((sides, meta_ref.shape[1] - slots), F32)], axis=1)
    row = lax.broadcasted_iota(jnp.int32, meta_ref.shape, 0)
    meta = jnp.where(row == sides, load_ref[0], 0).astype(F32)
    for side in range(sides):
        meta = jnp.where(row == side, lists[side : side + 1], meta)
    meta_ref[...] = meta.astype(BF16)
    tile_copy.wait()
    both = jnp.concatenate([tile_ref[0], tile_ref[1]], axis=1)
    for j in range(out_ref.shape[0]):
        out_ref[j] = both


def chunked(source, target, sems, dim, size):
    copies = []
    for j in range(source.shape[dim] // size):
        at = tuple(pl.ds(j * size, size) if d == dim else slice(None) for d in range(3))
        copies.append(pltpu.make_async_copy(source.at[at], target.at[at], sems.at[j]))
        copies[-1].start()
    return copies


def product(on_real, on_imag):
    k = on_real.shape[1] // 2
    return jnp.concatenate(
        [on_real[:, :k] - on_imag[:, k:], on_real[:, k:] + on_imag[:, :k]], axis=1
    )


def legs_kernel(tau_hbm, beta_hbm, tile_ref, out_ref, tau_ref, beta_ref, sems):
    parts, rows, _ = tile_ref.shape
    tau_copies = chunked(tau_hbm, tau_ref, sems.at[0], 2, rows)
    beta_copies = chunked(beta_hbm, beta_ref, sems.at[1], 1, rows)
    on_real = on_imag = None
    for j in range(parts):
        tau_copies[j].wait()
        add_real = dot(tau_ref[0, :, j * rows : (j + 1) * rows], tile_ref[j], 1, 0)
        add_imag = dot(tau_ref[1, :, j * rows : (j + 1) * rows], tile_ref[j], 1, 0)
        on_real = add_real if on_real is None else on_real + add_real
        on_imag = add_imag if on_imag is None else on_imag + add_imag
    image = product(on_real, on_imag).astype(BF16)
    for j in range(parts):
        beta_copies[j].wait()
        out_ref[j] = product(
            dot(beta_ref[0, j * rows : (j + 1) * rows, :], image, 1, 0),
            dot(beta_ref[1, j * rows : (j + 1) * rows, :], image, 1, 0),
        ).astype(BF16)


def pack_kernel(scale, meta_ref, parts_ref, sink_ref, out_ref):
    slices = out_ref.shape[0]
    k = sink_ref.shape[2]
    dressed = parts_ref[0].astype(F32)
    for j in range(1, parts_ref.shape[0]):
        dressed = dressed + parts_ref[j].astype(F32)
    dressed = dressed.astype(BF16)
    both = product(dot(sink_ref[0], dressed, 0, 0), -dot(sink_ref[1], dressed, 0, 0)) * scale
    real, imag = both[:, :k], both[:, k:]
    cut = [x.reshape(slices, k // slices, k) for x in (real.T, imag.T, real, imag)]
    packed = jnp.concatenate(cut, axis=1).astype(BF16)
    n = packed.shape[1]
    out_ref[:, :n, :] = packed
    for j in range(slices):
        out_ref[j, n:, :] = meta_ref[...]


def sum_kernel(ny, nc, in_ref, out_ref, numbers_ref):
    copies, pairs, rows, _ = out_ref.shape
    parts = in_ref.shape[0] // pairs
    tail = numbers_ref.shape[1]
    mine = lax.axis_index("c")
    for q in range(pairs):
        total = in_ref[q * parts, :rows, :].astype(F32)
        for j in range(1, parts):
            total = total + in_ref[q * parts + j, :rows, :].astype(F32)
        total = total.astype(BF16)
        for y in range(copies):
            out_ref[y, q] = total
        raw = in_ref[q * parts, rows:, :].astype(F32).astype(jnp.int32)[:tail]
        core, rest = raw & (nc - 1), raw >> (nc.bit_length() - 1)
        y, z = rest & (ny - 1), rest >> (ny.bit_length() - 1)
        place = jnp.where(core == mine, 0, ny * pairs) + y * pairs + z
        row = lax.broadcasted_iota(jnp.int32, raw.shape, 0)
        numbers_ref[q] = jnp.where(row < 2, place, raw)


def product_kernel(slots, scale, numbers_ref, own_ref, other_ref, out_ref, both_ref):
    owners, quarters, _, rows, k = out_ref.shape
    n = own_ref.shape[0]
    w = own_ref.shape[1] // 4
    both_ref[:n] = own_ref[...]
    both_ref[n:] = other_ref[...]
    for o in range(owners):
        load = numbers_ref[o, 2, 0]
        lefts, reals, imags = [], [], []
        for g in range(slots):
            left = both_ref[numbers_ref[o, 0, g], : 2 * w, :]
            right = both_ref[numbers_ref[o, 1, g], 2 * w :, :].astype(F32)
            lefts.append(jnp.where(g < load, left, jnp.zeros_like(left)))
            reals += [right[:w], -right[w:]]
            imags += [right[w:], right[:w]]
        left = jnp.concatenate(lefts, axis=0)
        right = jnp.concatenate(
            [jnp.concatenate(reals, axis=0), jnp.concatenate(imags, axis=0)], axis=1
        ).astype(BF16)
        total = dot(left, right, 0, 0) * scale
        for q in range(quarters):
            for c in range(2):
                out_ref[o, q, c] = total[q * rows : (q + 1) * rows, c * k : (c + 1) * k].astype(BF16)


def call(kernel, outs, specs, scratch=(), flops=0, moved=0, grant=16):
    outs = [jax.ShapeDtypeStruct(*out) for out in outs]
    return pl.pallas_call(
        kernel,
        out_shape=outs,
        in_specs=specs,
        out_specs=[VMEM] * len(outs),
        scratch_shapes=scratch,
        compiler_params=pltpu.CompilerParams(vmem_limit_bytes=grant * 2**20),
        cost_estimate=pl.CostEstimate(flops=flops, bytes_accessed=moved, transcendentals=0),
    )


def on_device(perambulator, backward, elementals, diagrams, owner_loads):
    tau = pltpu.with_memory_space_constraint(perambulator[0], pltpu.HBM)
    beta = pltpu.with_memory_space_constraint(backward[0], pltpu.HBM)
    tile = elementals[0, 0]
    lists = diagrams[0].T
    _, share, k = tile.shape
    order = tau.shape[2]
    nx, nz, ny, nc = (lax.axis_size(a) for a in ("blk", "z", "y", "c"))
    ns = lax.axis_size("sec")
    slots = diagrams.shape[1]
    slices = nz * nx
    w = k // slices
    quarter = k // nx

    before = lax.ppermute(tile, "sec", [((i - 1) % ns, i) for i in range(ns)])
    tiles, meta = call(
        spread_kernel,
        [((nx, share, 2 * k), BF16), ((16, k), BF16)],
        [HBM, HBM, SMEM],
        [
            pltpu.VMEM(tile.shape, BF16),
            pltpu.VMEM(lists.shape, jnp.int32),
            pltpu.SemaphoreType.DMA((2,)),
        ],
    )(
        pltpu.with_memory_space_constraint(tile, pltpu.HBM),
        pltpu.with_memory_space_constraint(lists, pltpu.HBM),
        owner_loads,
    )
    tiles = lax.all_to_all(tiles, "blk", 0, 0, tiled=True)
    (dressed,) = call(
        legs_kernel,
        [((nx, share, 2 * k), BF16)],
        [HBM, HBM, VMEM],
        [
            pltpu.VMEM(tau.shape, BF16),
            pltpu.VMEM(beta.shape, BF16),
            pltpu.SemaphoreType.DMA((2, nx)),
        ],
        16 * k * order * share,
        2**23,
    )(tau, beta, tiles)
    dressed = lax.all_to_all(dressed, "blk", 0, 0, tiled=True)
    (packed,) = call(
        lambda *refs: pack_kernel(order**-0.5, *refs), [((slices, 4 * w + 16, k), BF16)], [VMEM] * 3
    )(meta, dressed, before)
    packed = lax.all_to_all(packed, ("z", "blk"), 0, 0, tiled=True)
    pieces, numbers = call(
        lambda *refs: sum_kernel(ny, nc, *refs),
        [((ny, nz, 4 * w, k), BF16), ((nz, 8, k), jnp.int32)],
        [VMEM],
    )(packed)
    pieces = lax.all_to_all(pieces, "y", 0, 0, tiled=True)
    others = lax.ppermute(pieces, "c", [(i, (i + 1) % nc) for i in range(nc)])
    (partial,) = call(
        lambda *refs: product_kernel(slots, (k * slots) ** -0.5, *refs),
        [((nz, nx, 2, quarter, k), BF16)],
        [SMEM, VMEM, VMEM],
        [pltpu.VMEM((2 * ny * nz, 4 * w, k), BF16)],
    )(numbers, *(x.reshape(ny * nz, 4 * w, k) for x in (pieces, others)))
    arrived = lax.all_to_all(
        partial.reshape(slices, 2, quarter, k), ("z", "blk"), 0, 0, tiled=True
    )
    total = jnp.sum(arrived.astype(F32), axis=0)
    return total.reshape(1, 1, 2, quarter, k)


def solution(mesh):
    torus = Mesh(
        mesh.devices.reshape(mesh.shape["sec"], 4, 8, 2, mesh.shape["blk"]),
        ("sec", "z", "y", "c", "blk"),
    )
    in_specs = (
        P(TP, None, "blk", None),
        P(TP, None, None, "blk"),
        P("sec", TP, None, "blk", None),
        P(TP, None, None),
        P(TP),
    )
    out_specs = P("sec", TP, None, "blk", None)
    return jax.shard_map(
        on_device, mesh=torus, in_specs=in_specs, out_specs=out_specs, check_vma=False
    )
```

profile of v0, /device:TPU:1, one launch (start us, length us, event | category | flops | bytes accessed | tf_op | source)
XLA Modules:
  0.0 121.9 jit_solution(6799998412066825156)
XLA Ops:
  0.7 1.0 shard_map.55
  1.7 14.4 %all_to_all.25.tile_ref = bf16[4,512,256]{2,1,0:T(8,128)(2,1)S(1)} all-to-all(bf16[4,512,256]{2,1,0:T(8,128)(2,1)S(1)} %get-tuple-element.10), channel_id=1, replica_groups=mesh['sec'=3,'z'=4,'y'=8,'c'=2,'blk'=4] {'blk'}, dimensions={0} | all-to-all | bytes 2097152 | tf_op jit(solution)/shard_map/all_to_all | solution.py:184
  16.1 0.0 copy-start
  16.1 5.7 %shard_map.56 = bf16[4,512,256]{2,1,0:T(8,128)(2,1)} custom-call(bf16[2,512,2048]{2,1,0:T(8,128)(2,1)} %bitcast.13, bf16[2,2048,512]{2,1,0:T(8,128)(2,1)} %bitcast.14, bf16[4,512,256]{2,1,0:T(8,128)(2,1)S(1)} %all_to_all.25.tile_ref), custom_call_target="tpu_custom_call" | custom-call | flops 2147483648 | bytes 8388608 | tf_op jit(solution)/shard_map/pallas_call | solution.py:185
  21.8 3.5 %all-to-all-start.1 = ((bf16[4,512,256]{2,1,0:T(8,128)(2,1)}), bf16[4,512,256]{2,1,0:T(8,128)(2,1)S(1)}, u32[]{:S(2)}, u32[]{:S(2)}) async-start(bf16[4,512,256]{2,1,0:T(8,128)(2,1)} %shard_map.56), calls=%async_computation.1 | async-start | bytes 2097152 | tf_op jit(solution)/shard_map/all_to_all | solution.py:197
  25.4 0.0 copy-done
  25.4 15.1 %collective-permute-start = (bf16[2,512,128]{2,1,0:T(8,128)(2,1)S(1)}, bf16[2,512,128]{2,1,0:T(8,128)(2,1)S(1)}, u32[]{:S(2)}, u32[]{:S(2)}) collective-permute-start(bf16[2,512,128]{2,1,0:T(8,128)(2,1)S(1)} %bitcast.16), channel_id=1, source_target_pairs={{512,0},{0,256},{256,512},{513,1},{1,257},{257,513},{514,2},{2,258... | collective-permute-start | bytes 786440 | tf_op jit(solution)/shard_map/ppermute | solution.py:169
  40.5 8.7 %collective-permute-done.refs_2_ = bf16[2,512,128]{2,1,0:T(8,128)(2,1)S(1)} collective-permute-done((bf16[2,512,128]{2,1,0:T(8,128)(2,1)S(1)}, bf16[2,512,128]{2,1,0:T(8,128)(2,1)S(1)}, u32[]{:S(2)}, u32[]{:S(2)}) %collective-permute-start) | collective-permute-done | bytes 262176 | tf_op jit(solution)/shard_map/ppermute | solution.py:169
  49.2 0.0 all-to-all-done.1.refs_1_
  49.2 0.4 shard_map.57
  49.6 34.1 %all_to_all.26.refs_0_ = bf16[16,48,128]{2,1,0:T(8,128)(2,1)S(1)} all-to-all(bf16[16,48,128]{2,1,0:T(8,128)(2,1)S(1)} %shard_map.57), channel_id=1, replica_groups=mesh['sec'=3,'z'=4,'y'=8,'c'=2,'blk'=4] {'z','blk'}, dimensions={0} | all-to-all | bytes 393216 | tf_op jit(solution)/shard_map/all_to_all | solution.py:201
  83.7 16.1 %all_to_all.27 = bf16[8,4,32,128]{3,2,1,0:T(8,128)(2,1)S(1)} all-to-all(bf16[8,4,32,128]{3,2,1,0:T(8,128)(2,1)S(1)} %get-tuple-element.12), channel_id=1, replica_groups=mesh['sec'=3,'z'=4,'y'=8,'c'=2,'blk'=4] {'y'}, dimensions={0} | all-to-all | bytes 524288 | tf_op jit(solution)/shard_map/all_to_all | solution.py:207
  99.7 5.3 %collective-permute-start.1 = (bf16[8,4,32,128]{3,2,1,0:T(8,128)(2,1)S(1)}, bf16[8,4,32,128]{3,2,1,0:T(8,128)(2,1)S(1)}, u32[]{:S(2)}, u32[]{:S(2)}) collective-permute-start(bf16[8,4,32,128]{3,2,1,0:T(8,128)(2,1)S(1)} %all_to_all.27), channel_id=1, source_target_pairs={{0,4},{4,0},{1,5},{5,1},{2,6},{6,2},{3,7},{7,3},{8,12},{12,8},{9,1... | collective-permute-start | bytes 786440 | tf_op jit(solution)/shard_map/ppermute | solution.py:208
  105.0 1.1 collective-permute-done.1
  106.2 1.2 shard_map.59
  107.3 13.9 %all_to_all.28 = bf16[16,2,32,128]{3,2,1,0:T(8,128)(2,1)S(1)} all-to-all(bf16[16,2,32,128]{3,2,1,0:T(8,128)(2,1)S(1)} %bitcast.11), channel_id=1, replica_groups=mesh['sec'=3,'z'=4,'y'=8,'c'=2,'blk'=4] {'z','blk'}, dimensions={0} | all-to-all | bytes 524288 | tf_op jit(solution)/shard_map/all_to_all | solution.py:215
  121.2 0.7 convert_reduce_fusion
  (1 shorter events, 0.0 us)
Async XLA Ops:
  16.1 9.3 %copy-start = (bf16[1,1,2,512,128]{4,3,2,1,0:T(8,128)(2,1)S(1)}, bf16[1,1,2,512,128]{4,3,2,1,0:T(8,128)(2,1)}, u32[]{:S(2)}) copy-start(bf16[1,1,2,512,128]{4,3,2,1,0:T(8,128)(2,1)} %param.7) | copy-start | bytes 786436
  21.8 27.4 %all-to-all-start.1 = ((bf16[4,512,256]{2,1,0:T(8,128)(2,1)}), bf16[4,512,256]{2,1,0:T(8,128)(2,1)S(1)}, u32[]{:S(2)}, u32[]{:S(2)}) async-start(bf16[4,512,256]{2,1,0:T(8,128)(2,1)} %shard_map.56), calls=%async_computation.1 | async-start | bytes 2097152 | tf_op jit(solution)/shard_map/all_to_all | solution.py:197
  25.4 23.8 %collective-permute-start = (bf16[2,512,128]{2,1,0:T(8,128)(2,1)S(1)}, bf16[2,512,128]{2,1,0:T(8,128)(2,1)S(1)}, u32[]{:S(2)}, u32[]{:S(2)}) collective-permute-start(bf16[2,512,128]{2,1,0:T(8,128)(2,1)S(1)} %bitcast.16), channel_id=1, source_target_pairs={{512,0},{0,256},{256,512},{513,1},{1,257},{257,513},{514,2},{2,258... | collective-permute-start | bytes 786440 | tf_op jit(solution)/shard_map/ppermute | solution.py:169
  99.7 6.4 %collective-permute-start.1 = (bf16[8,4,32,128]{3,2,1,0:T(8,128)(2,1)S(1)}, bf16[8,4,32,128]{3,2,1,0:T(8,128)(2,1)S(1)}, u32[]{:S(2)}, u32[]{:S(2)}) collective-permute-start(bf16[8,4,32,128]{3,2,1,0:T(8,128)(2,1)S(1)} %all_to_all.27), channel_id=1, source_target_pairs={{0,4},{4,0},{1,5},{5,1},{2,6},{6,2},{3,7},{7,3},{8,12},{12,8},{9,1... | collective-permute-start | bytes 786440 | tf_op jit(solution)/shard_map/ppermute | solution.py:208
where the time goes:
time: 122 us
  blocking collectives  78.4 us (64%)
  starting transfers between devices  23.9 us (20%)
  waiting for transfers between devices  9.81 us (8%)
  Pallas kernels  8.36 us (7%)
    all_to_all x1, blocking collectives, on_device(): packed = lax.all_to_all(packed, ('z', 'blk'), 0, 0, tiled=True)  34.1 us
    all_to_all x1, blocking collectives, on_device(): pieces = lax.all_to_all(pieces, 'y', 0, 0, tiled=True)  16.1 us
    ppermute x1, starting transfers between devices, on_device(): before = lax.ppermute(tile, 'sec', [((i - 1) % ns, i) for i in range(ns)])  15.1 us
    all_to_all x1, blocking collectives, on_device(): tiles = lax.all_to_all(tiles, 'blk', 0, 0, tiled=True)  14.4 us
    all_to_all x1, blocking collectives, on_device(): lax.all_to_all(partial.reshape(slices, 2, quarter, k), ('z', 'blk'), 0, 0...  13.9 us
    ppermute x1, waiting for transfers between devices, on_device(): before = lax.ppermute(tile, 'sec', [((i - 1) % ns, i) for i in range(ns)])  8.67 us
    pallas_call x1, Pallas kernels, on_device(): call(legs_kernel, [((nx, share, 2 * k), BF16)], [HBM, HBM, VMEM], [pltpu....  5.75 us
    ppermute x1, starting transfers between devices, on_device(): others = lax.ppermute(pieces, 'c', [(i, (i + 1) % nc) for i in range(nc)])  5.27 us
  transfers between devices with their start and end apart: 3, of which 2 were waited for; matrix products, arithmetic and copies ran while one was open for 0% of the time, Pallas kernels for 0%

commit v1 on v0

--- a/solution.py
+++ b/solution.py
@@ -19,23 +19,10 @@
     return lax.dot_general(a, b, (((ca,), (cb,)), ((), ())), preferred_element_type=F32)
 
 
-def spread_kernel(
-    tile_hbm, lists_hbm, load_ref, out_ref, meta_ref, tile_ref, lists_ref, sems
-):
-    tile_copy = pltpu.make_async_copy(tile_hbm, tile_ref, sems.at[0])
-    lists_copy = pltpu.make_async_copy(lists_hbm, lists_ref, sems.at[1])
-    tile_copy.start()
-    lists_copy.start()
-    lists_copy.wait()
-    sides, slots = lists_ref.shape
-    lists = lists_ref[...].astype(F32)
-    lists = jnp.concatenate([lists, jnp.zeros((sides, meta_ref.shape[1] - slots), F32)], axis=1)
-    row = lax.broadcasted_iota(jnp.int32, meta_ref.shape, 0)
-    meta = jnp.where(row == sides, load_ref[0], 0).astype(F32)
-    for side in range(sides):
-        meta = jnp.where(row == side, lists[side : side + 1], meta)
-    meta_ref[...] = meta.astype(BF16)
-    tile_copy.wait()
+def spread_kernel(tile_hbm, out_ref, tile_ref, sem):
+    copy = pltpu.make_async_copy(tile_hbm, tile_ref, sem)
+    copy.start()
+    copy.wait()
     both = jnp.concatenate([tile_ref[0], tile_ref[1]], axis=1)
     for j in range(out_ref.shape[0]):
         out_ref[j] = both
@@ -57,10 +44,25 @@
     )
 
 
-def legs_kernel(tau_hbm, beta_hbm, tile_ref, out_ref, tau_ref, beta_ref, sems):
+def legs_kernel(
+    tau_hbm,
+    beta_hbm,
+    tile_ref,
+    lists_hbm,
+    load_ref,
+    out_ref,
+    meta_ref,
+    tau_ref,
+    beta_ref,
+    lists_ref,
+    sems,
+    lists_sem,
+):
     parts, rows, _ = tile_ref.shape
+    lists_copy = pltpu.make_async_copy(lists_hbm, lists_ref, lists_sem)
     tau_copies = chunked(tau_hbm, tau_ref, sems.at[0], 2, rows)
     beta_copies = chunked(beta_hbm, beta_ref, sems.at[1], 1, rows)
+    lists_copy.start()
     on_real = on_imag = None
     for j in range(parts):
         tau_copies[j].wait()
@@ -75,6 +77,15 @@
             dot(beta_ref[0, j * rows : (j + 1) * rows, :], image, 1, 0),
             dot(beta_ref[1, j * rows : (j + 1) * rows, :], image, 1, 0),
         ).astype(BF16)
+    lists_copy.wait()
+    sides, slots = lists_ref.shape
+    lists = lists_ref[...].astype(F32)
+    lists = jnp.concatenate([lists, jnp.zeros((sides, meta_ref.shape[1] - slots), F32)], axis=1)
+    row = lax.broadcasted_iota(jnp.int32, meta_ref.shape, 0)
+    meta = jnp.where(row == sides, load_ref[0], 0).astype(F32)
+    for side in range(sides):
+        meta = jnp.where(row == side, lists[side : side + 1], meta)
+    meta_ref[...] = meta.astype(BF16)
 
 
 def pack_kernel(scale, meta_ref, parts_ref, sink_ref, out_ref):
@@ -155,8 +166,8 @@
 def on_device(perambulator, backward, elementals, diagrams, owner_loads):
     tau = pltpu.with_memory_space_constraint(perambulator[0], pltpu.HBM)
     beta = pltpu.with_memory_space_constraint(backward[0], pltpu.HBM)
+    lists = pltpu.with_memory_space_constraint(diagrams[0].T, pltpu.HBM)
     tile = elementals[0, 0]
-    lists = diagrams[0].T
     _, share, k = tile.shape
     order = tau.shape[2]
     nx, nz, ny, nc = (lax.axis_size(a) for a in ("blk", "z", "y", "c"))
@@ -167,33 +178,27 @@
     quarter = k // nx
 
     before = lax.ppermute(tile, "sec", [((i - 1) % ns, i) for i in range(ns)])
-    tiles, meta = call(
+    (tiles,) = call(
         spread_kernel,
+        [((nx, share, 2 * k), BF16)],
+        [HBM],
+        [pltpu.VMEM(tile.shape, BF16), pltpu.SemaphoreType.DMA(())],
+    )(pltpu.with_memory_space_constraint(tile, pltpu.HBM))
+    tiles = lax.all_to_all(tiles, "blk", 0, 0, tiled=True)
+    dressed, meta = call(
+        legs_kernel,
         [((nx, share, 2 * k), BF16), ((16, k), BF16)],
-        [HBM, HBM, SMEM],
-        [
-            pltpu.VMEM(tile.shape, BF16),
-            pltpu.VMEM(lists.shape, jnp.int32),
-            pltpu.SemaphoreType.DMA((2,)),
-        ],
-    )(
-        pltpu.with_memory_space_constraint(tile, pltpu.HBM),
-        pltpu.with_memory_space_constraint(lists, pltpu.HBM),
-        owner_loads,
-    )
-    tiles = lax.all_to_all(tiles, "blk", 0, 0, tiled=True)
-    (dressed,) = call(
-        legs_kernel,
-        [((nx, share, 2 * k), BF16)],
-        [HBM, HBM, VMEM],
+        [HBM, HBM, VMEM, HBM, SMEM],
         [
             pltpu.VMEM(tau.shape, BF16),
             pltpu.VMEM(beta.shape, BF16),
+            pltpu.VMEM(lists.shape, jnp.int32),
             pltpu.SemaphoreType.DMA((2, nx)),
+            pltpu.SemaphoreType.DMA(()),
         ],
         16 * k * order * share,
         2**23,
-    )(tau, beta, tiles)
+    )(tau, beta, tiles, lists, owner_loads)
     dressed = lax.all_to_all(dressed, "blk", 0, 0, tiled=True)
     (packed,) = call(
         lambda *refs: pack_kernel(order**-0.5, *refs), [((slices, 4 * w + 16, k), BF16)], [VMEM] * 3

time: 122 us -> 123 us (level)
  blocking collectives: 78.4 us -> 64 us
  waiting for transfers between devices: 9.81 us -> 18.9 us
  starting transfers between devices: 23.9 us -> 28.8 us
    all_to_all x1 -> x0, blocking collectives: 14.4 us -> none  [on_device(): tiles = lax.all_to_all(tiles, 'blk', 0, 0, tiled=True)]
    all_to_all x0 -> x1, waiting for transfers between devices: none -> 9.09 us  [on_device(): tiles = lax.all_to_all(tiles, 'blk', 0, 0, tiled=True)]
    all_to_all x0 -> x1, starting transfers between devices: none -> 4.84 us  [on_device(): tiles = lax.all_to_all(tiles, 'blk', 0, 0, tiled=True)]
  transfers between devices with their start and end apart: 3 -> 4, of which waited for: 2 -> 3; matrix products, arithmetic and copies ran while one was open for 0% -> 0% of each run, Pallas kernels for 0% -> 0%
where the time goes in v1:
time: 123 us; the launch traced here: 122 us
  blocking collectives  64 us (52%)
  starting transfers between devices  28.8 us (23%)
  waiting for transfers between devices  18.9 us (15%)
  Pallas kernels  9.34 us (8%)
    all_to_all x1, blocking collectives, on_device(): packed = lax.all_to_all(packed, ('z', 'blk'), 0, 0, tiled=True)  34.1 us
    all_to_all x1, blocking collectives, on_device(): pieces = lax.all_to_all(pieces, 'y', 0, 0, tiled=True)  16.1 us
    ppermute x1, starting transfers between devices, on_device(): before = lax.ppermute(tile, 'sec', [((i - 1) % ns, i) for i in range(ns)])  15.1 us
    all_to_all x1, blocking collectives, on_device(): lax.all_to_all(partial.reshape(slices, 2, quarter, k), ('z', 'blk'), 0, 0...  13.9 us
    all_to_all x1, waiting for transfers between devices, on_device(): tiles = lax.all_to_all(tiles, 'blk', 0, 0, tiled=True)  9.09 us
    ppermute x1, waiting for transfers between devices, on_device(): before = lax.ppermute(tile, 'sec', [((i - 1) % ns, i) for i in range(ns)])  8.67 us
    pallas_call x1, Pallas kernels, on_device(): call(legs_kernel, [((nx, share, 2 * k), BF16), ((16, k), BF16)], [HBM, HB...  5.76 us
    ppermute x1, starting transfers between devices, on_device(): others = lax.ppermute(pieces, 'c', [(i, (i + 1) % nc) for i in range(nc)])  5.27 us
  transfers between devices with their start and end apart: 4, of which 3 were waited for; matrix products, arithmetic and copies ran while one was open for 0% of the time, Pallas kernels for 0%

profile of v1, /device:TPU:1, one launch (start us, length us, event | category | flops | bytes accessed | tf_op | source)
XLA Modules:
  0.0 122.4 jit_solution(18351738255258214161)
XLA Ops:
  0.0 2.0 %shard_map.55 = bf16[4,512,256]{2,1,0:T(8,128)(2,1)} custom-call(bf16[2,512,128]{2,1,0:T(8,128)(2,1)} %bitcast.15), custom_call_target="tpu_custom_call" | custom-call | tf_op jit(solution)/shard_map/pallas_call | solution.py:181
  2.0 4.8 %all-to-all-start = ((bf16[4,512,256]{2,1,0:T(8,128)(2,1)}), bf16[4,512,256]{2,1,0:T(8,128)(2,1)S(1)}, u32[]{:S(2)}, u32[]{:S(2)}) async-start(bf16[4,512,256]{2,1,0:T(8,128)(2,1)} %shard_map.55), calls=%async_computation | async-start | bytes 2097152 | tf_op jit(solution)/shard_map/all_to_all | solution.py:187
  7.5 9.1 %all-to-all-done.tile_ref = bf16[4,512,256]{2,1,0:T(8,128)(2,1)S(1)} async-done(((bf16[4,512,256]{2,1,0:T(8,128)(2,1)}), bf16[4,512,256]{2,1,0:T(8,128)(2,1)S(1)}, u32[]{:S(2)}, u32[]{:S(2)}) %all-to-all-start) | async-done | bytes 1048608 | tf_op jit(solution)/shard_map/all_to_all | solution.py:187
  16.6 0.0 copy-start
  16.6 5.8 %shard_map.56 = (bf16[4,512,256]{2,1,0:T(8,128)(2,1)}, bf16[16,128]{1,0:T(8,128)(2,1)S(1)}) custom-call(bf16[2,512,2048]{2,1,0:T(8,128)(2,1)} %bitcast.13, bf16[2,2048,512]{2,1,0:T(8,128)(2,1)} %bitcast.14, bf16[4,512,256]{2,1,0:T(8,128)(2,1)S(1)} %all-to-all-done.tile_ref, s32[2,16]{1,0:T(2,128)} %bitcast.17, s32[1]{0:T(128)S(6)} %copy.6.load_ref), custom_call_target="tpu_custom_call" | custom-call | flops 2147483648 | bytes 8388608 | tf_op jit(solution)/shard_map/pallas_call | solution.py:188
  22.4 3.5 %all-to-all-start.1 = ((bf16[4,512,256]{2,1,0:T(8,128)(2,1)}), bf16[4,512,256]{2,1,0:T(8,128)(2,1)S(1)}, u32[]{:S(2)}, u32[]{:S(2)}) async-start(bf16[4,512,256]{2,1,0:T(8,128)(2,1)} %get-tuple-element.10), calls=%async_computation.1 | async-start | bytes 2097152 | tf_op jit(solution)/shard_map/all_to_all | solution.py:202
  25.9 0.0 copy-done
  25.9 15.1 %collective-permute-start = (bf16[2,512,128]{2,1,0:T(8,128)(2,1)S(1)}, bf16[2,512,128]{2,1,0:T(8,128)(2,1)S(1)}, u32[]{:S(2)}, u32[]{:S(2)}) collective-permute-start(bf16[2,512,128]{2,1,0:T(8,128)(2,1)S(1)} %bitcast.16), channel_id=1, source_target_pairs={{512,0},{0,256},{256,512},{513,1},{1,257},{257,513},{514,2},{2,258... | collective-permute-start | bytes 786440 | tf_op jit(solution)/shard_map/ppermute | solution.py:180
  41.1 8.7 %collective-permute-done.refs_2_ = bf16[2,512,128]{2,1,0:T(8,128)(2,1)S(1)} collective-permute-done((bf16[2,512,128]{2,1,0:T(8,128)(2,1)S(1)}, bf16[2,512,128]{2,1,0:T(8,128)(2,1)S(1)}, u32[]{:S(2)}, u32[]{:S(2)}) %collective-permute-start) | collective-permute-done | bytes 262176 | tf_op jit(solution)/shard_map/ppermute | solution.py:180
  49.7 0.0 all-to-all-done.1.refs_1_
  49.7 0.4 shard_map.57
  50.1 34.1 %all_to_all.25.refs_0_ = bf16[16,48,128]{2,1,0:T(8,128)(2,1)S(1)} all-to-all(bf16[16,48,128]{2,1,0:T(8,128)(2,1)S(1)} %shard_map.57), channel_id=1, replica_groups=mesh['sec'=3,'z'=4,'y'=8,'c'=2,'blk'=4] {'z','blk'}, dimensions={0} | all-to-all | bytes 393216 | tf_op jit(solution)/shard_map/all_to_all | solution.py:206
  84.2 16.1 %all_to_all.26 = bf16[8,4,32,128]{3,2,1,0:T(8,128)(2,1)S(1)} all-to-all(bf16[8,4,32,128]{3,2,1,0:T(8,128)(2,1)S(1)} %get-tuple-element.12), channel_id=1, replica_groups=mesh['sec'=3,'z'=4,'y'=8,'c'=2,'blk'=4] {'y'}, dimensions={0} | all-to-all | bytes 524288 | tf_op jit(solution)/shard_map/all_to_all | solution.py:212
  100.3 5.3 %collective-permute-start.1 = (bf16[8,4,32,128]{3,2,1,0:T(8,128)(2,1)S(1)}, bf16[8,4,32,128]{3,2,1,0:T(8,128)(2,1)S(1)}, u32[]{:S(2)}, u32[]{:S(2)}) collective-permute-start(bf16[8,4,32,128]{3,2,1,0:T(8,128)(2,1)S(1)} %all_to_all.26), channel_id=1, source_target_pairs={{0,4},{4,0},{1,5},{5,1},{2,6},{6,2},{3,7},{7,3},{8,12},{12,8},{9,1... | collective-permute-start | bytes 786440 | tf_op jit(solution)/shard_map/ppermute | solution.py:213
  105.6 1.1 collective-permute-done.1
  106.7 1.2 shard_map.59
  107.9 13.9 %all_to_all.27 = bf16[16,2,32,128]{3,2,1,0:T(8,128)(2,1)S(1)} all-to-all(bf16[16,2,32,128]{3,2,1,0:T(8,128)(2,1)S(1)} %bitcast.11), channel_id=1, replica_groups=mesh['sec'=3,'z'=4,'y'=8,'c'=2,'blk'=4] {'z','blk'}, dimensions={0} | all-to-all | bytes 524288 | tf_op jit(solution)/shard_map/all_to_all | solution.py:220
  121.8 0.7 convert_reduce_fusion
  (1 shorter events, 0.0 us)
Async XLA Ops:
  2.0 14.6 %all-to-all-start = ((bf16[4,512,256]{2,1,0:T(8,128)(2,1)}), bf16[4,512,256]{2,1,0:T(8,128)(2,1)S(1)}, u32[]{:S(2)}, u32[]{:S(2)}) async-start(bf16[4,512,256]{2,1,0:T(8,128)(2,1)} %shard_map.55), calls=%async_computation | async-start | bytes 2097152 | tf_op jit(solution)/shard_map/all_to_all | solution.py:187
  16.6 9.3 %copy-start = (bf16[1,1,2,512,128]{4,3,2,1,0:T(8,128)(2,1)S(1)}, bf16[1,1,2,512,128]{4,3,2,1,0:T(8,128)(2,1)}, u32[]{:S(2)}) copy-start(bf16[1,1,2,512,128]{4,3,2,1,0:T(8,128)(2,1)} %param.7) | copy-start | bytes 786436
  22.4 27.4 %all-to-all-start.1 = ((bf16[4,512,256]{2,1,0:T(8,128)(2,1)}), bf16[4,512,256]{2,1,0:T(8,128)(2,1)S(1)}, u32[]{:S(2)}, u32[]{:S(2)}) async-start(bf16[4,512,256]{2,1,0:T(8,128)(2,1)} %get-tuple-element.10), calls=%async_computation.1 | async-start | bytes 2097152 | tf_op jit(solution)/shard_map/all_to_all | solution.py:202
  25.9 23.8 %collective-permute-start = (bf16[2,512,128]{2,1,0:T(8,128)(2,1)S(1)}, bf16[2,512,128]{2,1,0:T(8,128)(2,1)S(1)}, u32[]{:S(2)}, u32[]{:S(2)}) collective-permute-start(bf16[2,512,128]{2,1,0:T(8,128)(2,1)S(1)} %bitcast.16), channel_id=1, source_target_pairs={{512,0},{0,256},{256,512},{513,1},{1,257},{257,513},{514,2},{2,258... | collective-permute-start | bytes 786440 | tf_op jit(solution)/shard_map/ppermute | solution.py:180
  100.3 6.4 %collective-permute-start.1 = (bf16[8,4,32,128]{3,2,1,0:T(8,128)(2,1)S(1)}, bf16[8,4,32,128]{3,2,1,0:T(8,128)(2,1)S(1)}, u32[]{:S(2)}, u32[]{:S(2)}) collective-permute-start(bf16[8,4,32,128]{3,2,1,0:T(8,128)(2,1)S(1)} %all_to_all.26), channel_id=1, source_target_pairs={{0,4},{4,0},{1,5},{5,1},{2,6},{6,2},{3,7},{7,3},{8,12},{12,8},{9,1... | collective-permute-start | bytes 786440 | tf_op jit(solution)/shard_map/ppermute | solution.py:213

commit v2 on v0

--- a/solution.py
+++ b/solution.py
@@ -19,14 +19,42 @@
     return lax.dot_general(a, b, (((ca,), (cb,)), ((), ())), preferred_element_type=F32)
 
 
-def spread_kernel(
-    tile_hbm, lists_hbm, load_ref, out_ref, meta_ref, tile_ref, lists_ref, sems
+def product(on_real, on_imag):
+    k = on_real.shape[1] // 2
+    return jnp.concatenate(
+        [on_real[:, :k] - on_imag[:, k:], on_real[:, k:] + on_imag[:, :k]], axis=1
+    )
+
+
+def columns(tau_hbm, tau_ref, sems, chunk):
+    size = tau_hbm.shape[1]
+    at = pl.ds(pl.multiple_of(chunk * size, size), size)
+    return pltpu.make_async_copy(
+        tau_hbm.at[:, :, at], tau_ref.at[:, :, at], sems.at[chunk]
+    )
+
+
+def add_chunk(tau_ref, tile, chunk, total):
+    both = jnp.concatenate([tile[0], tile[1]], axis=1)
+    size = tau_ref.shape[1]
+    at = pl.ds(pl.multiple_of(chunk * size, size), size)
+    added = [dot(tau_ref[c, :, at], both, 1, 0) for c in range(2)]
+    return added if total is None else [x + y for x, y in zip(total, added)]
+
+
+def own_kernel(
+    tau_hbm, tile_hbm, lists_hbm, load_ref, total_ref, meta_ref, tau_ref, tile_ref, lists_ref, sems, small
 ):
-    tile_copy = pltpu.make_async_copy(tile_hbm, tile_ref, sems.at[0])
-    lists_copy = pltpu.make_async_copy(lists_hbm, lists_ref, sems.at[1])
-    tile_copy.start()
-    lists_copy.start()
-    lists_copy.wait()
+    own = lax.axis_index("blk")
+    copies = [
+        pltpu.make_async_copy(tile_hbm, tile_ref, small.at[0]),
+        pltpu.make_async_copy(lists_hbm, lists_ref, small.at[1]),
+        columns(tau_hbm, tau_ref, sems, own),
+    ]
+    for copy in copies:
+        copy.start()
+    for copy in copies:
+        copy.wait()
     sides, slots = lists_ref.shape
     lists = lists_ref[...].astype(F32)
     lists = jnp.concatenate([lists, jnp.zeros((sides, meta_ref.shape[1] - slots), F32)], axis=1)
@@ -35,46 +63,43 @@
     for side in range(sides):
         meta = jnp.where(row == side, lists[side : side + 1], meta)
     meta_ref[...] = meta.astype(BF16)
-    tile_copy.wait()
-    both = jnp.concatenate([tile_ref[0], tile_ref[1]], axis=1)
-    for j in range(out_ref.shape[0]):
-        out_ref[j] = both
-
-
-def chunked(source, target, sems, dim, size):
-    copies = []
-    for j in range(source.shape[dim] // size):
-        at = tuple(pl.ds(j * size, size) if d == dim else slice(None) for d in range(3))
-        copies.append(pltpu.make_async_copy(source.at[at], target.at[at], sems.at[j]))
-        copies[-1].start()
-    return copies
-
-
-def product(on_real, on_imag):
-    k = on_real.shape[1] // 2
-    return jnp.concatenate(
-        [on_real[:, :k] - on_imag[:, k:], on_real[:, k:] + on_imag[:, :k]], axis=1
-    )
-
-
-def legs_kernel(tau_hbm, beta_hbm, tile_ref, out_ref, tau_ref, beta_ref, sems):
-    parts, rows, _ = tile_ref.shape
-    tau_copies = chunked(tau_hbm, tau_ref, sems.at[0], 2, rows)
-    beta_copies = chunked(beta_hbm, beta_ref, sems.at[1], 1, rows)
-    on_real = on_imag = None
-    for j in range(parts):
-        tau_copies[j].wait()
-        add_real = dot(tau_ref[0, :, j * rows : (j + 1) * rows], tile_ref[j], 1, 0)
-        add_imag = dot(tau_ref[1, :, j * rows : (j + 1) * rows], tile_ref[j], 1, 0)
-        on_real = add_real if on_real is None else on_real + add_real
-        on_imag = add_imag if on_imag is None else on_imag + add_imag
-    image = product(on_real, on_imag).astype(BF16)
+    total_ref[0], total_ref[1] = add_chunk(tau_ref, tile_ref[...], own, None)
+
+
+def legs_kernel(
+    tau_hbm, beta_hbm, tile_ref, own_ref, out_hbm, tau_ref, beta_ref, out_ref, sems
+):
+    parts, _, rows, _ = tile_ref.shape
+    own = lax.axis_index("blk")
+    others = [lax.rem(own + j, parts) for j in range(1, parts)]
+    for chunk in others:
+        columns(tau_hbm, tau_ref, sems.at[0], chunk).start()
+    beta_copies = [
+        pltpu.make_async_copy(
+            beta_hbm.at[:, pl.ds(j * rows, rows), :],
+            beta_ref.at[:, pl.ds(j * rows, rows), :],
+            sems.at[1, j],
+        )
+        for j in range(parts)
+    ]
+    for copy in beta_copies:
+        copy.start()
+    total = [own_ref[0], own_ref[1]]
+    for chunk in others:
+        columns(tau_hbm, tau_ref, sems.at[0], chunk).wait()
+        total = add_chunk(tau_ref, tile_ref[chunk], chunk, total)
+    image = product(*total).astype(BF16)
+    out_copies = []
     for j in range(parts):
         beta_copies[j].wait()
         out_ref[j] = product(
             dot(beta_ref[0, j * rows : (j + 1) * rows, :], image, 1, 0),
             dot(beta_ref[1, j * rows : (j + 1) * rows, :], image, 1, 0),
         ).astype(BF16)
+        out_copies.append(pltpu.make_async_copy(out_ref.at[j], out_hbm.at[j], sems.at[2, j]))
+        out_copies[-1].start()
+    for copy in out_copies:
+        copy.wait()
 
 
 def pack_kernel(scale, meta_ref, parts_ref, sink_ref, out_ref):
@@ -139,13 +164,13 @@
                 out_ref[o, q, c] = total[q * rows : (q + 1) * rows, c * k : (c + 1) * k].astype(BF16)
 
 
-def call(kernel, outs, specs, scratch=(), flops=0, moved=0, grant=16):
+def call(kernel, outs, specs, scratch=(), flops=0, moved=0, grant=16, out=VMEM):
     outs = [jax.ShapeDtypeStruct(*out) for out in outs]
     return pl.pallas_call(
         kernel,
         out_shape=outs,
         in_specs=specs,
-        out_specs=[VMEM] * len(outs),
+        out_specs=[out] * len(outs),
         scratch_shapes=scratch,
         compiler_params=pltpu.CompilerParams(vmem_limit_bytes=grant * 2**20),
         cost_estimate=pl.CostEstimate(flops=flops, bytes_accessed=moved, transcendentals=0),
@@ -155,8 +180,8 @@
 def on_device(perambulator, backward, elementals, diagrams, owner_loads):
     tau = pltpu.with_memory_space_constraint(perambulator[0], pltpu.HBM)
     beta = pltpu.with_memory_space_constraint(backward[0], pltpu.HBM)
+    lists = pltpu.with_memory_space_constraint(diagrams[0].T, pltpu.HBM)
     tile = elementals[0, 0]
-    lists = diagrams[0].T
     _, share, k = tile.shape
     order = tau.shape[2]
     nx, nz, ny, nc = (lax.axis_size(a) for a in ("blk", "z", "y", "c"))
@@ -167,33 +192,35 @@
     quarter = k // nx
 
     before = lax.ppermute(tile, "sec", [((i - 1) % ns, i) for i in range(ns)])
-    tiles, meta = call(
-        spread_kernel,
-        [((nx, share, 2 * k), BF16), ((16, k), BF16)],
-        [HBM, HBM, SMEM],
+    tiles = lax.all_to_all(jnp.broadcast_to(tile[None], (nx, *tile.shape)), "blk", 0, 0, tiled=True)
+    total, meta = call(
+        own_kernel,
+        [((2, share, 2 * k), F32), ((16, k), BF16)],
+        [HBM, HBM, HBM, SMEM],
         [
+            pltpu.VMEM(tau.shape, BF16),
             pltpu.VMEM(tile.shape, BF16),
             pltpu.VMEM(lists.shape, jnp.int32),
+            pltpu.SemaphoreType.DMA((nx,)),
             pltpu.SemaphoreType.DMA((2,)),
         ],
-    )(
-        pltpu.with_memory_space_constraint(tile, pltpu.HBM),
-        pltpu.with_memory_space_constraint(lists, pltpu.HBM),
-        owner_loads,
-    )
-    tiles = lax.all_to_all(tiles, "blk", 0, 0, tiled=True)
+        8 * k * share * share,
+        2**20,
+    )(tau, pltpu.with_memory_space_constraint(tile, pltpu.HBM), lists, owner_loads)
     (dressed,) = call(
         legs_kernel,
         [((nx, share, 2 * k), BF16)],
-        [HBM, HBM, VMEM],
+        [HBM, HBM, VMEM, VMEM],
         [
             pltpu.VMEM(tau.shape, BF16),
             pltpu.VMEM(beta.shape, BF16),
-            pltpu.SemaphoreType.DMA((2, nx)),
+            pltpu.VMEM((nx, share, 2 * k), BF16),
+            pltpu.SemaphoreType.DMA((3, nx)),
         ],
         16 * k * order * share,
         2**23,
-    )(tau, beta, tiles)
+        out=HBM,
+    )(tau, beta, tiles, total)
     dressed = lax.all_to_all(dressed, "blk", 0, 0, tiled=True)
     (packed,) = call(
         lambda *refs: pack_kernel(order**-0.5, *refs), [((slices, 4 * w + 16, k), BF16)], [VMEM] * 3

time: 122 us -> 122 us (level)
  blocking collectives: 78.4 us -> 64 us
  waiting for transfers between devices: 9.81 us -> 17.1 us
  starting transfers between devices: 23.9 us -> 28.8 us
  local copies, waits for them, and re-layouts: 0.01 us -> 2.06 us
    all_to_all x1 -> x0, blocking collectives: 14.4 us -> none  [on_device(): tiles = lax.all_to_all(tiles, 'blk', 0, 0, tiled=True)]
    all_to_all x0 -> x1, waiting for transfers between devices: none -> 7.26 us  [on_device(): lax.all_to_all(jnp.broadcast_to(tile[None], (nx, *tile.shape)), 'blk', 0,...]
    all_to_all x0 -> x1, starting transfers between devices: none -> 4.83 us  [on_device(): lax.all_to_all(jnp.broadcast_to(tile[None], (nx, *tile.shape)), 'blk', 0,...]
    broadcast_in_dim x0 -> x1, local copies, waits for them, and re-layouts: none -> 2.06 us  [on_device(): jnp.broadcast_to(tile[None], (nx, *tile.shape))]
  transfers between devices with their start and end apart: 3 -> 4, of which waited for: 2 -> 3; matrix products, arithmetic and copies ran while one was open for 0% -> 0% of each run, Pallas kernels for 0% -> 2%
where the time goes in v2:
time: 122 us
  blocking collectives  64 us (52%)
  starting transfers between devices  28.8 us (24%)
  waiting for transfers between devices  17.1 us (14%)
  Pallas kernels  8.33 us (7%)
  local copies, waits for them, and re-layouts  2.06 us (2%)
    all_to_all x1, blocking collectives, on_device(): packed = lax.all_to_all(packed, ('z', 'blk'), 0, 0, tiled=True)  34.1 us
    all_to_all x1, blocking collectives, on_device(): pieces = lax.all_to_all(pieces, 'y', 0, 0, tiled=True)  16.1 us
    ppermute x1, starting transfers between devices, on_device(): before = lax.ppermute(tile, 'sec', [((i - 1) % ns, i) for i in range(ns)])  15.1 us
    all_to_all x1, blocking collectives, on_device(): lax.all_to_all(partial.reshape(slices, 2, quarter, k), ('z', 'blk'), 0, 0...  13.9 us
    ppermute x1, waiting for transfers between devices, on_device(): before = lax.ppermute(tile, 'sec', [((i - 1) % ns, i) for i in range(ns)])  8.67 us
    all_to_all x1, waiting for transfers between devices, on_device(): lax.all_to_all(jnp.broadcast_to(tile[None], (nx, *tile.shape)), 'blk', 0,...  7.26 us
    ppermute x1, starting transfers between devices, on_device(): others = lax.ppermute(pieces, 'c', [(i, (i + 1) % nc) for i in range(nc)])  5.27 us
    pallas_call x1, Pallas kernels, on_device(): call(legs_kernel, [((nx, share, 2 * k), BF16)], [HBM, HBM, VMEM, VMEM], [...  4.93 us
  transfers between devices with their start and end apart: 4, of which 3 were waited for; matrix products, arithmetic and copies ran while one was open for 0% of the time, Pallas kernels for 2%

profile of v2, /device:TPU:1, one launch (start us, length us, event | category | flops | bytes accessed | tf_op | source)
XLA Modules:
  0.0 121.6 jit_solution(12207116811388028009)
XLA Ops:
  0.0 2.1 %broadcast_in_dim.2 = bf16[4,2,512,128]{3,2,1,0:T(8,128)(2,1)} broadcast(bf16[2,512,128]{2,1,0:T(8,128)(2,1)} %bitcast.16), dimensions={1,2,3} | broadcast | bytes 1310720 | tf_op jit(solution)/shard_map/broadcast_in_dim | solution.py:195
  2.1 4.8 %all-to-all-start = ((bf16[4,2,512,128]{3,2,1,0:T(8,128)(2,1)}), bf16[4,2,512,128]{3,2,1,0:T(8,128)(2,1)S(1)}, u32[]{:S(2)}, u32[]{:S(2)}) async-start(bf16[4,2,512,128]{3,2,1,0:T(8,128)(2,1)} %broadcast_in_dim.2), calls=%async_computation | async-start | bytes 2097152 | tf_op jit(solution)/shard_map/all_to_all | solution.py:195
  7.5 1.8 %shard_map.55 = (f32[2,512,256]{2,1,0:T(8,128)S(1)}, bf16[16,128]{1,0:T(8,128)(2,1)S(1)}) custom-call(bf16[2,512,2048]{2,1,0:T(8,128)(2,1)} %bitcast.13, bf16[2,512,128]{2,1,0:T(8,128)(2,1)} %bitcast.17, s32[2,16]{1,0:T(2,128)} %bitcast.19, s32[1]{0:T(128)S(6)} %copy.6.load_ref), custom_call_target="tpu_custom_call" | custom-call | flops 268435456 | bytes 1048576 | tf_op jit(solution)/shard_map/pallas_call | solution.py:196
  9.4 7.3 %all-to-all-done.tile_ref = bf16[4,2,512,128]{3,2,1,0:T(8,128)(2,1)S(1)} async-done(((bf16[4,2,512,128]{3,2,1,0:T(8,128)(2,1)}), bf16[4,2,512,128]{3,2,1,0:T(8,128)(2,1)S(1)}, u32[]{:S(2)}, u32[]{:S(2)}) %all-to-all-start) | async-done | bytes 1048608 | tf_op jit(solution)/shard_map/all_to_all | solution.py:195
  16.6 0.0 copy-start
  16.6 4.9 %shard_map.56 = bf16[4,512,256]{2,1,0:T(8,128)(2,1)} custom-call(bf16[2,512,2048]{2,1,0:T(8,128)(2,1)} %bitcast.14, bf16[2,2048,512]{2,1,0:T(8,128)(2,1)} %bitcast.15, bf16[4,2,512,128]{3,2,1,0:T(8,128)(2,1)S(1)} %all-to-all-done.tile_ref, f32[2,512,256]{2,1,0:T(8,128)S(1)} %get-tuple-element.10.own_ref), custom_call_target="tpu_custom_call" | custom-call | flops 2147483648 | bytes 8388608 | tf_op jit(solution)/shard_map/pallas_call | solution.py:210
  21.6 3.5 %all-to-all-start.1 = ((bf16[4,512,256]{2,1,0:T(8,128)(2,1)}), bf16[4,512,256]{2,1,0:T(8,128)(2,1)S(1)}, u32[]{:S(2)}, u32[]{:S(2)}) async-start(bf16[4,512,256]{2,1,0:T(8,128)(2,1)} %shard_map.56), calls=%async_computation.1 | async-start | bytes 2097152 | tf_op jit(solution)/shard_map/all_to_all | solution.py:224
  25.1 0.0 copy-done
  25.1 15.1 %collective-permute-start = (bf16[2,512,128]{2,1,0:T(8,128)(2,1)S(1)}, bf16[2,512,128]{2,1,0:T(8,128)(2,1)S(1)}, u32[]{:S(2)}, u32[]{:S(2)}) collective-permute-start(bf16[2,512,128]{2,1,0:T(8,128)(2,1)S(1)} %bitcast.18), channel_id=1, source_target_pairs={{512,0},{0,256},{256,512},{513,1},{1,257},{257,513},{514,2},{2,258... | collective-permute-start | bytes 786440 | tf_op jit(solution)/shard_map/ppermute | solution.py:194
  40.3 8.7 %collective-permute-done.refs_2_ = bf16[2,512,128]{2,1,0:T(8,128)(2,1)S(1)} collective-permute-done((bf16[2,512,128]{2,1,0:T(8,128)(2,1)S(1)}, bf16[2,512,128]{2,1,0:T(8,128)(2,1)S(1)}, u32[]{:S(2)}, u32[]{:S(2)}) %collective-permute-start) | collective-permute-done | bytes 262176 | tf_op jit(solution)/shard_map/ppermute | solution.py:194
  48.9 0.0 all-to-all-done.1.refs_1_
  48.9 0.4 shard_map.57
  49.3 34.1 %all_to_all.25.refs_0_ = bf16[16,48,128]{2,1,0:T(8,128)(2,1)S(1)} all-to-all(bf16[16,48,128]{2,1,0:T(8,128)(2,1)S(1)} %shard_map.57), channel_id=1, replica_groups=mesh['sec'=3,'z'=4,'y'=8,'c'=2,'blk'=4] {'z','blk'}, dimensions={0} | all-to-all | bytes 393216 | tf_op jit(solution)/shard_map/all_to_all | solution.py:228
  83.4 16.1 %all_to_all.26 = bf16[8,4,32,128]{3,2,1,0:T(8,128)(2,1)S(1)} all-to-all(bf16[8,4,32,128]{3,2,1,0:T(8,128)(2,1)S(1)} %get-tuple-element.12), channel_id=1, replica_groups=mesh['sec'=3,'z'=4,'y'=8,'c'=2,'blk'=4] {'y'}, dimensions={0} | all-to-all | bytes 524288 | tf_op jit(solution)/shard_map/all_to_all | solution.py:234
  99.5 5.3 %collective-permute-start.1 = (bf16[8,4,32,128]{3,2,1,0:T(8,128)(2,1)S(1)}, bf16[8,4,32,128]{3,2,1,0:T(8,128)(2,1)S(1)}, u32[]{:S(2)}, u32[]{:S(2)}) collective-permute-start(bf16[8,4,32,128]{3,2,1,0:T(8,128)(2,1)S(1)} %all_to_all.26), channel_id=1, source_target_pairs={{0,4},{4,0},{1,5},{5,1},{2,6},{6,2},{3,7},{7,3},{8,12},{12,8},{9,1... | collective-permute-start | bytes 786440 | tf_op jit(solution)/shard_map/ppermute | solution.py:235
  104.8 1.1 collective-permute-done.1
  105.9 1.2 shard_map.59
  107.1 13.9 %all_to_all.27 = bf16[16,2,32,128]{3,2,1,0:T(8,128)(2,1)S(1)} all-to-all(bf16[16,2,32,128]{3,2,1,0:T(8,128)(2,1)S(1)} %bitcast.11), channel_id=1, replica_groups=mesh['sec'=3,'z'=4,'y'=8,'c'=2,'blk'=4] {'z','blk'}, dimensions={0} | all-to-all | bytes 524288 | tf_op jit(solution)/shard_map/all_to_all | solution.py:242
  121.0 0.7 convert_reduce_fusion
  (1 shorter events, 0.0 us)
Async XLA Ops:
  2.1 14.6 %all-to-all-start = ((bf16[4,2,512,128]{3,2,1,0:T(8,128)(2,1)}), bf16[4,2,512,128]{3,2,1,0:T(8,128)(2,1)S(1)}, u32[]{:S(2)}, u32[]{:S(2)}) async-start(bf16[4,2,512,128]{3,2,1,0:T(8,128)(2,1)} %broadcast_in_dim.2), calls=%async_computation | async-start | bytes 2097152 | tf_op jit(solution)/shard_map/all_to_all | solution.py:195
  16.6 8.5 %copy-start = (bf16[1,1,2,512,128]{4,3,2,1,0:T(8,128)(2,1)S(1)}, bf16[1,1,2,512,128]{4,3,2,1,0:T(8,128)(2,1)}, u32[]{:S(2)}) copy-start(bf16[1,1,2,512,128]{4,3,2,1,0:T(8,128)(2,1)} %param.7) | copy-start | bytes 786436
  21.6 27.4 %all-to-all-start.1 = ((bf16[4,512,256]{2,1,0:T(8,128)(2,1)}), bf16[4,512,256]{2,1,0:T(8,128)(2,1)S(1)}, u32[]{:S(2)}, u32[]{:S(2)}) async-start(bf16[4,512,256]{2,1,0:T(8,128)(2,1)} %shard_map.56), calls=%async_computation.1 | async-start | bytes 2097152 | tf_op jit(solution)/shard_map/all_to_all | solution.py:224
  25.1 23.8 %collective-permute-start = (bf16[2,512,128]{2,1,0:T(8,128)(2,1)S(1)}, bf16[2,512,128]{2,1,0:T(8,128)(2,1)S(1)}, u32[]{:S(2)}, u32[]{:S(2)}) collective-permute-start(bf16[2,512,128]{2,1,0:T(8,128)(2,1)S(1)} %bitcast.18), channel_id=1, source_target_pairs={{512,0},{0,256},{256,512},{513,1},{1,257},{257,513},{514,2},{2,258... | collective-permute-start | bytes 786440 | tf_op jit(solution)/shard_map/ppermute | solution.py:194
  99.5 6.4 %collective-permute-start.1 = (bf16[8,4,32,128]{3,2,1,0:T(8,128)(2,1)S(1)}, bf16[8,4,32,128]{3,2,1,0:T(8,128)(2,1)S(1)}, u32[]{:S(2)}, u32[]{:S(2)}) collective-permute-start(bf16[8,4,32,128]{3,2,1,0:T(8,128)(2,1)S(1)} %all_to_all.26), channel_id=1, source_target_pairs={{0,4},{4,0},{1,5},{5,1},{2,6},{6,2},{3,7},{7,3},{8,12},{12,8},{9,1... | collective-permute-start | bytes 786440 | tf_op jit(solution)/shard_map/ppermute | solution.py:235

commit v3 on v2

--- a/solution.py
+++ b/solution.py
@@ -26,6 +26,20 @@
     )
 
 
+def spread_kernel(tile_hbm, out_hbm, tile_ref, sems):
+    parts = out_hbm.shape[0]
+    copy = pltpu.make_async_copy(tile_hbm, tile_ref, sems.at[parts])
+    copy.start()
+    copy.wait()
+    copies = [
+        pltpu.make_async_copy(tile_ref, out_hbm.at[j], sems.at[j]) for j in range(parts)
+    ]
+    for copy in copies:
+        copy.start()
+    for copy in copies:
+        copy.wait()
+
+
 def columns(tau_hbm, tau_ref, sems, chunk):
     size = tau_hbm.shape[1]
     at = pl.ds(pl.multiple_of(chunk * size, size), size)
@@ -43,13 +57,26 @@
 
 
 def own_kernel(
-    tau_hbm, tile_hbm, lists_hbm, load_ref, total_ref, meta_ref, tau_ref, tile_ref, lists_ref, sems, small
+    tau_hbm,
+    beta_hbm,
+    tile_hbm,
+    lists_hbm,
+    load_ref,
+    total_ref,
+    beta_ref,
+    meta_ref,
+    tau_ref,
+    tile_ref,
+    lists_ref,
+    sems,
+    small,
 ):
     own = lax.axis_index("blk")
     copies = [
         pltpu.make_async_copy(tile_hbm, tile_ref, small.at[0]),
         pltpu.make_async_copy(lists_hbm, lists_ref, small.at[1]),
         columns(tau_hbm, tau_ref, sems, own),
+        pltpu.make_async_copy(beta_hbm.at[:, pl.ds(0, beta_ref.shape[1]), :], beta_ref, small.at[2]),
     ]
     for copy in copies:
         copy.start()
@@ -67,7 +94,7 @@
 
 
 def legs_kernel(
-    tau_hbm, beta_hbm, tile_ref, own_ref, out_hbm, tau_ref, beta_ref, out_ref, sems
+    tau_hbm, beta_hbm, tile_ref, own_ref, first_ref, out_hbm, tau_ref, beta_ref, out_ref, sems
 ):
     parts, _, rows, _ = tile_ref.shape
     own = lax.axis_index("blk")
@@ -76,26 +103,22 @@
         columns(tau_hbm, tau_ref, sems.at[0], chunk).start()
     beta_copies = [
         pltpu.make_async_copy(
-            beta_hbm.at[:, pl.ds(j * rows, rows), :],
-            beta_ref.at[:, pl.ds(j * rows, rows), :],
-            sems.at[1, j],
+            beta_hbm.at[:, pl.ds(j * rows, rows), :], beta_ref.at[j - 1], sems.at[1, j]
         )
-        for j in range(parts)
+        for j in range(1, parts)
     ]
-    for copy in beta_copies:
+    total = [own_ref[0], own_ref[1]]
+    for chunk, copy in zip(others, beta_copies):
+        columns(tau_hbm, tau_ref, sems.at[0], chunk).wait()
         copy.start()
-    total = [own_ref[0], own_ref[1]]
-    for chunk in others:
-        columns(tau_hbm, tau_ref, sems.at[0], chunk).wait()
         total = add_chunk(tau_ref, tile_ref[chunk], chunk, total)
     image = product(*total).astype(BF16)
     out_copies = []
     for j in range(parts):
-        beta_copies[j].wait()
-        out_ref[j] = product(
-            dot(beta_ref[0, j * rows : (j + 1) * rows, :], image, 1, 0),
-            dot(beta_ref[1, j * rows : (j + 1) * rows, :], image, 1, 0),
-        ).astype(BF16)
+        if j > 0:
+            beta_copies[j - 1].wait()
+        beta = first_ref if j == 0 else beta_ref.at[j - 1]
+        out_ref[j] = product(dot(beta[0], image, 1, 0), dot(beta[1], image, 1, 0)).astype(BF16)
         out_copies.append(pltpu.make_async_copy(out_ref.at[j], out_hbm.at[j], sems.at[2, j]))
         out_copies[-1].start()
     for copy in out_copies:
@@ -192,35 +215,43 @@
     quarter = k // nx
 
     before = lax.ppermute(tile, "sec", [((i - 1) % ns, i) for i in range(ns)])
-    tiles = lax.all_to_all(jnp.broadcast_to(tile[None], (nx, *tile.shape)), "blk", 0, 0, tiled=True)
-    total, meta = call(
+    tile_hbm = pltpu.with_memory_space_constraint(tile, pltpu.HBM)
+    (tiles,) = call(
+        spread_kernel,
+        [((nx, *tile.shape), BF16)],
+        [HBM],
+        [pltpu.VMEM(tile.shape, BF16), pltpu.SemaphoreType.DMA((nx + 1,))],
+        out=HBM,
+    )(tile_hbm)
+    tiles = lax.all_to_all(tiles, "blk", 0, 0, tiled=True)
+    total, beta_first, meta = call(
         own_kernel,
-        [((2, share, 2 * k), F32), ((16, k), BF16)],
-        [HBM, HBM, HBM, SMEM],
+        [((2, share, 2 * k), F32), ((2, share, share), BF16), ((16, k), BF16)],
+        [HBM, HBM, HBM, HBM, SMEM],
         [
             pltpu.VMEM(tau.shape, BF16),
             pltpu.VMEM(tile.shape, BF16),
             pltpu.VMEM(lists.shape, jnp.int32),
             pltpu.SemaphoreType.DMA((nx,)),
-            pltpu.SemaphoreType.DMA((2,)),
+            pltpu.SemaphoreType.DMA((3,)),
         ],
         8 * k * share * share,
         2**20,
-    )(tau, pltpu.with_memory_space_constraint(tile, pltpu.HBM), lists, owner_loads)
+    )(tau, beta, tile_hbm, lists, owner_loads)
     (dressed,) = call(
         legs_kernel,
         [((nx, share, 2 * k), BF16)],
-        [HBM, HBM, VMEM, VMEM],
+        [HBM, HBM, VMEM, VMEM, VMEM],
         [
             pltpu.VMEM(tau.shape, BF16),
-            pltpu.VMEM(beta.shape, BF16),
+            pltpu.VMEM((nx - 1, 2, share, share), BF16),
             pltpu.VMEM((nx, share, 2 * k), BF16),
             pltpu.SemaphoreType.DMA((3, nx)),
         ],
         16 * k * order * share,
         2**23,
         out=HBM,
-    )(tau, beta, tiles, total)
+    )(tau, beta, tiles, total, beta_first)
     dressed = lax.all_to_all(dressed, "blk", 0, 0, tiled=True)
     (packed,) = call(
         lambda *refs: pack_kernel(order**-0.5, *refs), [((slices, 4 * w + 16, k), BF16)], [VMEM] * 3

time: 122 us -> 122 us (level)
  Pallas kernels: 8.33 us -> 10.9 us
  local copies, waits for them, and re-layouts: 2.06 us -> 0.01 us
    pallas_call x2 -> x3, Pallas kernels: 6.76 us -> 9.37 us  [the longest x1 5.26 us: on_device(): call(legs_kernel, [((nx, share, 2 * k), BF16)], [HBM, HBM, VMEM, VMEM, VM...]
    broadcast_in_dim x1 -> x0, local copies, waits for them, and re-layouts: 2.06 us -> none  [on_device(): jnp.broadcast_to(tile[None], (nx, *tile.shape))]
where the time goes in v3:
time: 122 us
  blocking collectives  64 us (52%)
  starting transfers between devices  28.8 us (24%)
  waiting for transfers between devices  16.7 us (14%)
  Pallas kernels  10.9 us (9%)
    all_to_all x1, blocking collectives, on_device(): packed = lax.all_to_all(packed, ('z', 'blk'), 0, 0, tiled=True)  34.1 us
    all_to_all x1, blocking collectives, on_device(): pieces = lax.all_to_all(pieces, 'y', 0, 0, tiled=True)  16.1 us
    ppermute x1, starting transfers between devices, on_device(): before = lax.ppermute(tile, 'sec', [((i - 1) % ns, i) for i in range(ns)])  15.1 us
    all_to_all x1, blocking collectives, on_device(): lax.all_to_all(partial.reshape(slices, 2, quarter, k), ('z', 'blk'), 0, 0...  13.9 us
    ppermute x1, waiting for transfers between devices, on_device(): before = lax.ppermute(tile, 'sec', [((i - 1) % ns, i) for i in range(ns)])  8.67 us
    all_to_all x1, waiting for transfers between devices, on_device(): tiles = lax.all_to_all(tiles, 'blk', 0, 0, tiled=True)  6.93 us
    ppermute x1, starting transfers between devices, on_device(): others = lax.ppermute(pieces, 'c', [(i, (i + 1) % nc) for i in range(nc)])  5.32 us
    pallas_call x1, Pallas kernels, on_device(): call(legs_kernel, [((nx, share, 2 * k), BF16)], [HBM, HBM, VMEM, VMEM, VM...  5.26 us
  transfers between devices with their start and end apart: 4, of which 3 were waited for; matrix products, arithmetic and copies ran while one was open for 0% of the time, Pallas kernels for 2%

profile of v3, /device:TPU:1, one launch (start us, length us, event | category | flops | bytes accessed | tf_op | source)
XLA Modules:
  0.0 121.9 jit_solution(5629749193246379818)
XLA Ops:
  0.0 2.0 %shard_map.56 = bf16[4,2,512,128]{3,2,1,0:T(8,128)(2,1)} custom-call(bf16[2,512,128]{2,1,0:T(8,128)(2,1)} %bitcast.17), custom_call_target="tpu_custom_call" | custom-call | tf_op jit(solution)/shard_map/pallas_call | solution.py:219
  2.0 4.8 %all-to-all-start = ((bf16[4,2,512,128]{3,2,1,0:T(8,128)(2,1)}), bf16[4,2,512,128]{3,2,1,0:T(8,128)(2,1)S(1)}, u32[]{:S(2)}, u32[]{:S(2)}) async-start(bf16[4,2,512,128]{3,2,1,0:T(8,128)(2,1)} %shard_map.56), calls=%async_computation | async-start | bytes 2097152 | tf_op jit(solution)/shard_map/all_to_all | solution.py:226
  7.5 2.2 %shard_map.55 = (f32[2,512,256]{2,1,0:T(8,128)S(1)}, bf16[2,512,512]{2,1,0:T(8,128)(2,1)S(1)}, bf16[16,128]{1,0:T(8,128)(2,1)S(1)}) custom-call(bf16[2,512,2048]{2,1,0:T(8,128)(2,1)} %bitcast.13, bf16[2,2048,512]{2,1,0:T(8,128)(2,1)} %bitcast.15, bf16[2,512,128]{2,1,0:T(8,128)(2,1)} %bitcast.18, s32[2,16]{1,0:T(2,128)} %bitcast.20, s32[1]{0:T(128)S(6)} %copy.6.load_ref), custom_call_target="tpu_custom_call" | custom-call | flops 268435456 | bytes 1048576 | tf_op jit(solution)/shard_map/pallas_call | solution.py:227
  9.6 6.9 %all-to-all-done.tile_ref = bf16[4,2,512,128]{3,2,1,0:T(8,128)(2,1)S(1)} async-done(((bf16[4,2,512,128]{3,2,1,0:T(8,128)(2,1)}), bf16[4,2,512,128]{3,2,1,0:T(8,128)(2,1)S(1)}, u32[]{:S(2)}, u32[]{:S(2)}) %all-to-all-start) | async-done | bytes 1048608 | tf_op jit(solution)/shard_map/all_to_all | solution.py:226
  16.6 0.0 copy-start
  16.6 5.3 %shard_map.57 = bf16[4,512,256]{2,1,0:T(8,128)(2,1)} custom-call(bf16[2,512,2048]{2,1,0:T(8,128)(2,1)} %bitcast.14, bf16[2,2048,512]{2,1,0:T(8,128)(2,1)} %bitcast.16, bf16[4,2,512,128]{3,2,1,0:T(8,128)(2,1)S(1)} %all-to-all-done.tile_ref, f32[2,512,256]{2,1,0:T(8,128)S(1)} %get-tuple-element.11.own_ref, bf16[2,512,512]{2,1,0:T(8,128)(2,1)S(1)} %get-tuple-element.12.first_ref), custom_call_target="tpu_custom_call" | custom-call | flops 2147483648 | bytes 8388608 | tf_op jit(solution)/shard_map/pallas_call | solution.py:241
  21.8 3.5 %all-to-all-start.1 = ((bf16[4,512,256]{2,1,0:T(8,128)(2,1)}), bf16[4,512,256]{2,1,0:T(8,128)(2,1)S(1)}, u32[]{:S(2)}, u32[]{:S(2)}) async-start(bf16[4,512,256]{2,1,0:T(8,128)(2,1)} %shard_map.57), calls=%async_computation.1 | async-start | bytes 2097152 | tf_op jit(solution)/shard_map/all_to_all | solution.py:255
  25.4 0.0 copy-done
  25.4 15.1 %collective-permute-start = (bf16[2,512,128]{2,1,0:T(8,128)(2,1)S(1)}, bf16[2,512,128]{2,1,0:T(8,128)(2,1)S(1)}, u32[]{:S(2)}, u32[]{:S(2)}) collective-permute-start(bf16[2,512,128]{2,1,0:T(8,128)(2,1)S(1)} %bitcast.19), channel_id=1, source_target_pairs={{512,0},{0,256},{256,512},{513,1},{1,257},{257,513},{514,2},{2,258... | collective-permute-start | bytes 786440 | tf_op jit(solution)/shard_map/ppermute | solution.py:217
  40.5 8.7 %collective-permute-done.refs_2_ = bf16[2,512,128]{2,1,0:T(8,128)(2,1)S(1)} collective-permute-done((bf16[2,512,128]{2,1,0:T(8,128)(2,1)S(1)}, bf16[2,512,128]{2,1,0:T(8,128)(2,1)S(1)}, u32[]{:S(2)}, u32[]{:S(2)}) %collective-permute-start) | collective-permute-done | bytes 262176 | tf_op jit(solution)/shard_map/ppermute | solution.py:217
  49.2 0.0 all-to-all-done.1.refs_1_
  49.2 0.4 shard_map.58
  49.6 34.1 %all_to_all.25.refs_0_ = bf16[16,48,128]{2,1,0:T(8,128)(2,1)S(1)} all-to-all(bf16[16,48,128]{2,1,0:T(8,128)(2,1)S(1)} %shard_map.58), channel_id=1, replica_groups=mesh['sec'=3,'z'=4,'y'=8,'c'=2,'blk'=4] {'z','blk'}, dimensions={0} | all-to-all | bytes 393216 | tf_op jit(solution)/shard_map/all_to_all | solution.py:259
  83.7 16.1 %all_to_all.26 = bf16[8,4,32,128]{3,2,1,0:T(8,128)(2,1)S(1)} all-to-all(bf16[8,4,32,128]{3,2,1,0:T(8,128)(2,1)S(1)} %get-tuple-element.14), channel_id=1, replica_groups=mesh['sec'=3,'z'=4,'y'=8,'c'=2,'blk'=4] {'y'}, dimensions={0} | all-to-all | bytes 524288 | tf_op jit(solution)/shard_map/all_to_all | solution.py:265
  99.7 5.3 %collective-permute-start.1 = (bf16[8,4,32,128]{3,2,1,0:T(8,128)(2,1)S(1)}, bf16[8,4,32,128]{3,2,1,0:T(8,128)(2,1)S(1)}, u32[]{:S(2)}, u32[]{:S(2)}) collective-permute-start(bf16[8,4,32,128]{3,2,1,0:T(8,128)(2,1)S(1)} %all_to_all.26), channel_id=1, source_target_pairs={{0,4},{4,0},{1,5},{5,1},{2,6},{6,2},{3,7},{7,3},{8,12},{12,8},{9,1... | collective-permute-start | bytes 786440 | tf_op jit(solution)/shard_map/ppermute | solution.py:266
  105.0 1.1 collective-permute-done.1
  106.2 1.2 shard_map.60
  107.3 13.9 %all_to_all.27 = bf16[16,2,32,128]{3,2,1,0:T(8,128)(2,1)S(1)} all-to-all(bf16[16,2,32,128]{3,2,1,0:T(8,128)(2,1)S(1)} %bitcast.11), channel_id=1, replica_groups=mesh['sec'=3,'z'=4,'y'=8,'c'=2,'blk'=4] {'z','blk'}, dimensions={0} | all-to-all | bytes 524288 | tf_op jit(solution)/shard_map/all_to_all | solution.py:273
  121.2 0.7 convert_reduce_fusion
  (1 shorter events, 0.0 us)
Async XLA Ops:
  2.0 14.6 %all-to-all-start = ((bf16[4,2,512,128]{3,2,1,0:T(8,128)(2,1)}), bf16[4,2,512,128]{3,2,1,0:T(8,128)(2,1)S(1)}, u32[]{:S(2)}, u32[]{:S(2)}) async-start(bf16[4,2,512,128]{3,2,1,0:T(8,128)(2,1)} %shard_map.56), calls=%async_computation | async-start | bytes 2097152 | tf_op jit(solution)/shard_map/all_to_all | solution.py:226
  16.6 8.8 %copy-start = (bf16[1,1,2,512,128]{4,3,2,1,0:T(8,128)(2,1)S(1)}, bf16[1,1,2,512,128]{4,3,2,1,0:T(8,128)(2,1)}, u32[]{:S(2)}) copy-start(bf16[1,1,2,512,128]{4,3,2,1,0:T(8,128)(2,1)} %param.7) | copy-start | bytes 786436
  21.8 27.3 %all-to-all-start.1 = ((bf16[4,512,256]{2,1,0:T(8,128)(2,1)}), bf16[4,512,256]{2,1,0:T(8,128)(2,1)S(1)}, u32[]{:S(2)}, u32[]{:S(2)}) async-start(bf16[4,512,256]{2,1,0:T(8,128)(2,1)} %shard_map.57), calls=%async_computation.1 | async-start | bytes 2097152 | tf_op jit(solution)/shard_map/all_to_all | solution.py:255
  25.4 23.8 %collective-permute-start = (bf16[2,512,128]{2,1,0:T(8,128)(2,1)S(1)}, bf16[2,512,128]{2,1,0:T(8,128)(2,1)S(1)}, u32[]{:S(2)}, u32[]{:S(2)}) collective-permute-start(bf16[2,512,128]{2,1,0:T(8,128)(2,1)S(1)} %bitcast.19), channel_id=1, source_target_pairs={{512,0},{0,256},{256,512},{513,1},{1,257},{257,513},{514,2},{2,258... | collective-permute-start | bytes 786440 | tf_op jit(solution)/shard_map/ppermute | solution.py:217
  99.7 6.5 %collective-permute-start.1 = (bf16[8,4,32,128]{3,2,1,0:T(8,128)(2,1)S(1)}, bf16[8,4,32,128]{3,2,1,0:T(8,128)(2,1)S(1)}, u32[]{:S(2)}, u32[]{:S(2)}) collective-permute-start(bf16[8,4,32,128]{3,2,1,0:T(8,128)(2,1)S(1)} %all_to_all.26), channel_id=1, source_target_pairs={{0,4},{4,0},{1,5},{5,1},{2,6},{6,2},{3,7},{7,3},{8,12},{12,8},{9,1... | collective-permute-start | bytes 786440 | tf_op jit(solution)/shard_map/ppermute | solution.py:266

commit v4 on v3

--- a/solution.py
+++ b/solution.py
@@ -107,10 +107,11 @@
         )
         for j in range(1, parts)
     ]
+    for copy in beta_copies:
+        copy.start()
     total = [own_ref[0], own_ref[1]]
-    for chunk, copy in zip(others, beta_copies):
+    for chunk in others:
         columns(tau_hbm, tau_ref, sems.at[0], chunk).wait()
-        copy.start()
         total = add_chunk(tau_ref, tile_ref[chunk], chunk, total)
     image = product(*total).astype(BF16)
     out_copies = []
@@ -226,7 +227,7 @@
     tiles = lax.all_to_all(tiles, "blk", 0, 0, tiled=True)
     total, beta_first, meta = call(
         own_kernel,
-        [((2, share, 2 * k), F32), ((2, share, share), BF16), ((16, k), BF16)],
+        [((2, share, 2 * k), F32), ((2, share, share), BF16), ((8, k), BF16)],
         [HBM, HBM, HBM, HBM, SMEM],
         [
             pltpu.VMEM(tau.shape, BF16),
@@ -254,7 +255,7 @@
     )(tau, beta, tiles, total, beta_first)
     dressed = lax.all_to_all(dressed, "blk", 0, 0, tiled=True)
     (packed,) = call(
-        lambda *refs: pack_kernel(order**-0.5, *refs), [((slices, 4 * w + 16, k), BF16)], [VMEM] * 3
+        lambda *refs: pack_kernel(order**-0.5, *refs), [((slices, 4 * w + 8, k), BF16)], [VMEM] * 3
     )(meta, dressed, before)
     packed = lax.all_to_all(packed, ("z", "blk"), 0, 0, tiled=True)
     pieces, numbers = call(

time: 122 us -> 121 us (level)
  no operation moved by 1% of the time
where the time goes in v4:
time: 121 us
  blocking collectives  63.4 us (52%)
  starting transfers between devices  28.7 us (24%)
  waiting for transfers between devices  16.7 us (14%)
  Pallas kernels  10.5 us (9%)
    all_to_all x1, blocking collectives, on_device(): packed = lax.all_to_all(packed, ('z', 'blk'), 0, 0, tiled=True)  33.5 us
    all_to_all x1, blocking collectives, on_device(): pieces = lax.all_to_all(pieces, 'y', 0, 0, tiled=True)  16.1 us
    ppermute x1, starting transfers between devices, on_device(): before = lax.ppermute(tile, 'sec', [((i - 1) % ns, i) for i in range(ns)])  15.1 us
    all_to_all x1, blocking collectives, on_device(): lax.all_to_all(partial.reshape(slices, 2, quarter, k), ('z', 'blk'), 0, 0...  13.8 us
    ppermute x1, waiting for transfers between devices, on_device(): before = lax.ppermute(tile, 'sec', [((i - 1) % ns, i) for i in range(ns)])  8.67 us
    all_to_all x1, waiting for transfers between devices, on_device(): tiles = lax.all_to_all(tiles, 'blk', 0, 0, tiled=True)  6.93 us
    ppermute x1, starting transfers between devices, on_device(): others = lax.ppermute(pieces, 'c', [(i, (i + 1) % nc) for i in range(nc)])  5.23 us
    pallas_call x1, Pallas kernels, on_device(): call(legs_kernel, [((nx, share, 2 * k), BF16)], [HBM, HBM, VMEM, VMEM, VM...  4.85 us
  transfers between devices with their start and end apart: 4, of which 3 were waited for; matrix products, arithmetic and copies ran while one was open for 0% of the time, Pallas kernels for 2%

profile of v4, /device:TPU:1, one launch (start us, length us, event | category | flops | bytes accessed | tf_op | source)
XLA Modules:
  0.0 120.8 jit_solution(11740634076555708012)
XLA Ops:
  0.0 2.0 %shard_map.56 = bf16[4,2,512,128]{3,2,1,0:T(8,128)(2,1)} custom-call(bf16[2,512,128]{2,1,0:T(8,128)(2,1)} %bitcast.17), custom_call_target="tpu_custom_call" | custom-call | tf_op jit(solution)/shard_map/pallas_call | solution.py:220
  2.0 4.8 %all-to-all-start = ((bf16[4,2,512,128]{3,2,1,0:T(8,128)(2,1)}), bf16[4,2,512,128]{3,2,1,0:T(8,128)(2,1)S(1)}, u32[]{:S(2)}, u32[]{:S(2)}) async-start(bf16[4,2,512,128]{3,2,1,0:T(8,128)(2,1)} %shard_map.56), calls=%async_computation | async-start | bytes 2097152 | tf_op jit(solution)/shard_map/all_to_all | solution.py:227
  7.5 2.2 %shard_map.55 = (f32[2,512,256]{2,1,0:T(8,128)S(1)}, bf16[2,512,512]{2,1,0:T(8,128)(2,1)S(1)}, bf16[8,128]{1,0:T(8,128)(2,1)S(1)}) custom-call(bf16[2,512,2048]{2,1,0:T(8,128)(2,1)} %bitcast.13, bf16[2,2048,512]{2,1,0:T(8,128)(2,1)} %bitcast.15, bf16[2,512,128]{2,1,0:T(8,128)(2,1)} %bitcast.18, s32[2,16]{1,0:T(2,128)} %bitcast.20, s32[1]{0:T(128)S(6)} %copy.6.load_ref), custom_call_target="tpu_custom_call" | custom-call | flops 268435456 | bytes 1048576 | tf_op jit(solution)/shard_map/pallas_call | solution.py:228
  9.6 6.9 %all-to-all-done.tile_ref = bf16[4,2,512,128]{3,2,1,0:T(8,128)(2,1)S(1)} async-done(((bf16[4,2,512,128]{3,2,1,0:T(8,128)(2,1)}), bf16[4,2,512,128]{3,2,1,0:T(8,128)(2,1)S(1)}, u32[]{:S(2)}, u32[]{:S(2)}) %all-to-all-start) | async-done | bytes 1048608 | tf_op jit(solution)/shard_map/all_to_all | solution.py:227
  16.6 0.0 copy-start
  16.6 4.8 %shard_map.57 = bf16[4,512,256]{2,1,0:T(8,128)(2,1)} custom-call(bf16[2,512,2048]{2,1,0:T(8,128)(2,1)} %bitcast.14, bf16[2,2048,512]{2,1,0:T(8,128)(2,1)} %bitcast.16, bf16[4,2,512,128]{3,2,1,0:T(8,128)(2,1)S(1)} %all-to-all-done.tile_ref, f32[2,512,256]{2,1,0:T(8,128)S(1)} %get-tuple-element.11.own_ref, bf16[2,512,512]{2,1,0:T(8,128)(2,1)S(1)} %get-tuple-element.12.first_ref), custom_call_target="tpu_custom_call" | custom-call | flops 2147483648 | bytes 8388608 | tf_op jit(solution)/shard_map/pallas_call | solution.py:242
  21.4 3.5 %all-to-all-start.1 = ((bf16[4,512,256]{2,1,0:T(8,128)(2,1)}), bf16[4,512,256]{2,1,0:T(8,128)(2,1)S(1)}, u32[]{:S(2)}, u32[]{:S(2)}) async-start(bf16[4,512,256]{2,1,0:T(8,128)(2,1)} %shard_map.57), calls=%async_computation.1 | async-start | bytes 2097152 | tf_op jit(solution)/shard_map/all_to_all | solution.py:256
  25.0 0.0 copy-done
  25.0 15.1 %collective-permute-start = (bf16[2,512,128]{2,1,0:T(8,128)(2,1)S(1)}, bf16[2,512,128]{2,1,0:T(8,128)(2,1)S(1)}, u32[]{:S(2)}, u32[]{:S(2)}) collective-permute-start(bf16[2,512,128]{2,1,0:T(8,128)(2,1)S(1)} %bitcast.19), channel_id=1, source_target_pairs={{512,0},{0,256},{256,512},{513,1},{1,257},{257,513},{514,2},{2,258... | collective-permute-start | bytes 786440 | tf_op jit(solution)/shard_map/ppermute | solution.py:218
  40.1 8.7 %collective-permute-done.refs_2_ = bf16[2,512,128]{2,1,0:T(8,128)(2,1)S(1)} collective-permute-done((bf16[2,512,128]{2,1,0:T(8,128)(2,1)S(1)}, bf16[2,512,128]{2,1,0:T(8,128)(2,1)S(1)}, u32[]{:S(2)}, u32[]{:S(2)}) %collective-permute-start) | collective-permute-done | bytes 262176 | tf_op jit(solution)/shard_map/ppermute | solution.py:218
  48.8 0.0 all-to-all-done.1.refs_1_
  48.8 0.4 shard_map.58
  49.1 33.5 %all_to_all.25.refs_0_ = bf16[16,40,128]{2,1,0:T(8,128)(2,1)S(1)} all-to-all(bf16[16,40,128]{2,1,0:T(8,128)(2,1)S(1)} %shard_map.58), channel_id=1, replica_groups=mesh['sec'=3,'z'=4,'y'=8,'c'=2,'blk'=4] {'z','blk'}, dimensions={0} | all-to-all | bytes 327680 | tf_op jit(solution)/shard_map/all_to_all | solution.py:260
  82.7 16.1 %all_to_all.26 = bf16[8,4,32,128]{3,2,1,0:T(8,128)(2,1)S(1)} all-to-all(bf16[8,4,32,128]{3,2,1,0:T(8,128)(2,1)S(1)} %get-tuple-element.14), channel_id=1, replica_groups=mesh['sec'=3,'z'=4,'y'=8,'c'=2,'blk'=4] {'y'}, dimensions={0} | all-to-all | bytes 524288 | tf_op jit(solution)/shard_map/all_to_all | solution.py:266
  98.8 5.2 %collective-permute-start.1 = (bf16[8,4,32,128]{3,2,1,0:T(8,128)(2,1)S(1)}, bf16[8,4,32,128]{3,2,1,0:T(8,128)(2,1)S(1)}, u32[]{:S(2)}, u32[]{:S(2)}) collective-permute-start(bf16[8,4,32,128]{3,2,1,0:T(8,128)(2,1)S(1)} %all_to_all.26), channel_id=1, source_target_pairs={{0,4},{4,0},{1,5},{5,1},{2,6},{6,2},{3,7},{7,3},{8,12},{12,8},{9,1... | collective-permute-start | bytes 786440 | tf_op jit(solution)/shard_map/ppermute | solution.py:267
  104.1 1.1 collective-permute-done.1
  105.2 1.2 shard_map.60
  106.4 13.8 %all_to_all.27 = bf16[16,2,32,128]{3,2,1,0:T(8,128)(2,1)S(1)} all-to-all(bf16[16,2,32,128]{3,2,1,0:T(8,128)(2,1)S(1)} %bitcast.11), channel_id=1, replica_groups=mesh['sec'=3,'z'=4,'y'=8,'c'=2,'blk'=4] {'z','blk'}, dimensions={0} | all-to-all | bytes 524288 | tf_op jit(solution)/shard_map/all_to_all | solution.py:274
  120.1 0.7 convert_reduce_fusion
  (1 shorter events, 0.0 us)
Async XLA Ops:
  2.0 14.6 %all-to-all-start = ((bf16[4,2,512,128]{3,2,1,0:T(8,128)(2,1)}), bf16[4,2,512,128]{3,2,1,0:T(8,128)(2,1)S(1)}, u32[]{:S(2)}, u32[]{:S(2)}) async-start(bf16[4,2,512,128]{3,2,1,0:T(8,128)(2,1)} %shard_map.56), calls=%async_computation | async-start | bytes 2097152 | tf_op jit(solution)/shard_map/all_to_all | solution.py:227
  16.6 8.4 %copy-start = (bf16[1,1,2,512,128]{4,3,2,1,0:T(8,128)(2,1)S(1)}, bf16[1,1,2,512,128]{4,3,2,1,0:T(8,128)(2,1)}, u32[]{:S(2)}) copy-start(bf16[1,1,2,512,128]{4,3,2,1,0:T(8,128)(2,1)} %param.7) | copy-start | bytes 786436
  21.4 27.3 %all-to-all-start.1 = ((bf16[4,512,256]{2,1,0:T(8,128)(2,1)}), bf16[4,512,256]{2,1,0:T(8,128)(2,1)S(1)}, u32[]{:S(2)}, u32[]{:S(2)}) async-start(bf16[4,512,256]{2,1,0:T(8,128)(2,1)} %shard_map.57), calls=%async_computation.1 | async-start | bytes 2097152 | tf_op jit(solution)/shard_map/all_to_all | solution.py:256
  25.0 23.8 %collective-permute-start = (bf16[2,512,128]{2,1,0:T(8,128)(2,1)S(1)}, bf16[2,512,128]{2,1,0:T(8,128)(2,1)S(1)}, u32[]{:S(2)}, u32[]{:S(2)}) collective-permute-start(bf16[2,512,128]{2,1,0:T(8,128)(2,1)S(1)} %bitcast.19), channel_id=1, source_target_pairs={{512,0},{0,256},{256,512},{513,1},{1,257},{257,513},{514,2},{2,258... | collective-permute-start | bytes 786440 | tf_op jit(solution)/shard_map/ppermute | solution.py:218
  98.8 6.4 %collective-permute-start.1 = (bf16[8,4,32,128]{3,2,1,0:T(8,128)(2,1)S(1)}, bf16[8,4,32,128]{3,2,1,0:T(8,128)(2,1)S(1)}, u32[]{:S(2)}, u32[]{:S(2)}) collective-permute-start(bf16[8,4,32,128]{3,2,1,0:T(8,128)(2,1)S(1)} %all_to_all.26), channel_id=1, source_target_pairs={{0,4},{4,0},{1,5},{5,1},{2,6},{6,2},{3,7},{7,3},{8,12},{12,8},{9,1... | collective-permute-start | bytes 786440 | tf_op jit(solution)/shard_map/ppermute | solution.py:267
